TPU v7x, 32 devices: a whole 2x2x4 slice. The times are simulated.
32 devices in a mesh: dp: 4 (over y, x), tensor: 2 (over core), expert: 4 (over z).
Axes of the slice: x: 2, y: 2, z: 4, core: 2. Of those that a mesh axis runs over, the one named last changes fastest.
Arguments:
- tokens: bfloat16 [2048, 2304], P(('dp', 'tensor', 'expert')), may hold values from -6 to 6
- routes: int32 [2048, 2], P(('dp', 'tensor', 'expert')), may hold values from 0 to 7, all different within a row; in each aligned block of 64 rows (0 to 63, 64 to 127, ...) at most 24 rows name the same one
- gates: float32 [2048, 2], P(('dp', 'tensor', 'expert')), may hold values from 0.2 to 1
- segments: int32 [2048], P(('dp', 'tensor', 'expert')), may hold values from 0 to 7, never falling along the last dimension, each value on 1 to 512 neighbouring positions
- w_gate: bfloat16 [8, 2304, 7680], P('expert', None, ('dp', 'tensor')), may hold values from -0.125 to 0.125
- w_up: bfloat16 [8, 2304, 7680], P('expert', None, ('dp', 'tensor')), may hold values from -0.125 to 0.125
- w_down: bfloat16 [8, 7680, 2304], P('expert', ('dp', 'tensor')), may hold values from -0.0625 to 0.0625
Outputs:
- embedded: bfloat16 [2048, 2304], P(('dp', 'tensor', 'expert'))
- pooled: float32 [8, 2304], replicated
Inputs may be any that keep to these rules, and one draw needn't show every extreme that they name: `routes`: each residue names two different experts. Within the rows of one device no expert is named more than 24 times, and in every draw some expert is named exactly 24 times by the rows of some device. `segments`: sequence numbers never fall along the residues; each sequence has 1 to 512 residues and one has exactly 512.
All inputs are finite; a program needn't handle non-finite values.
Results may differ from a plain program's by a relative error of at most 0.0085.
Values may be sent and summed in bfloat16 or wider, within the bound.
No kernel may reach another device: no remote copies, remote signals or barrier semaphores. Data moves between devices by JAX's collectives and lax.ppermute only.
A program may use at most 128 MiB of HBM per device.

v0:
```python
import jax
import jax.numpy as jnp
from jax import lax
from jax.sharding import PartitionSpec as P

EXPERTS = 8
TOP = 2
CAP = 24
epsilon = 1e-06


def norm_tokens(tokens):
    values = tokens.astype(jnp.float32)
    scale = lax.rsqrt(jnp.mean(values * values, axis=1, keepdims=True) + epsilon)
    return (values, (values * scale).astype(jnp.bfloat16))


def slot_numbers(routes):
    flat_routes = routes.reshape(-1)
    onehot = (flat_routes[:, None] == jnp.arange(EXPERTS, dtype=jnp.int32)[None, :]).astype(
        jnp.int32
    )
    before = jnp.cumsum(onehot, axis=0) - onehot
    slot_rank = jnp.sum(before * onehot, axis=1)
    return flat_routes * CAP + slot_rank


def placement_matrix(slot_index, tok_count):
    hits = (jnp.arange(EXPERTS * CAP, dtype=jnp.int32)[:, None] == slot_index[None, :]).astype(
        jnp.int32
    )
    return jnp.sum(hits.reshape(EXPERTS * CAP, tok_count, TOP), axis=2).astype(jnp.bfloat16)


def fan_out(slot_rows, replicas):
    leading = slot_rows.shape[:-2]
    features = slot_rows.shape[-1]
    shaped = slot_rows.reshape(leading + (EXPERTS, CAP, features))
    if replicas > 1:
        shaped = jnp.repeat(shaped, replicas, axis=len(leading))
    return shaped.reshape(leading + (EXPERTS * replicas * CAP, features))


def expert_hidden(row_block, w_gate, w_up):
    gate_proj = jnp.einsum("nacd,adf->nacf", row_block, w_gate, preferred_element_type=jnp.float32)
    up_proj = jnp.einsum("nacd,adf->nacf", row_block, w_up, preferred_element_type=jnp.float32)
    return (jax.nn.silu(gate_proj) * up_proj).astype(jnp.bfloat16)


def shards(tokens, routes, gates, segments, w_gate, w_up, w_down):
    tok_count = tokens.shape[0]
    width = tokens.shape[1]
    experts_axis = lax.axis_size("expert")
    per_device = w_gate.shape[0]
    replicas = max(1, experts_axis // EXPERTS)
    plane = lax.axis_size("dp") * lax.axis_size("tensor")
    values, normed = norm_tokens(tokens)
    slot_index = slot_numbers(routes)
    placing = placement_matrix(slot_index, tok_count)
    slot_rows = jnp.dot(placing, normed, preferred_element_type=jnp.float32).astype(jnp.bfloat16)
    send_rows = fan_out(slot_rows, replicas)
    received = lax.all_to_all(send_rows, "expert", split_axis=0, concat_axis=0, tiled=True)
    local_rows = received.reshape(experts_axis, per_device, CAP, width)
    hidden = expert_hidden(
        lax.all_gather(local_rows, ("dp", "tensor"), axis=0, tiled=True), w_gate, w_up
    )
    summed = lax.psum_scatter(
        jnp.einsum("nacf,afd->nacd", hidden, w_down, preferred_element_type=jnp.float32).astype(
            jnp.bfloat16
        ),
        ("dp", "tensor"),
        scatter_dimension=0,
        tiled=True,
    )
    returned = lax.all_to_all(summed, "expert", split_axis=0, concat_axis=0, tiled=True).astype(
        jnp.float32
    )
    if replicas > 1:
        expert_out = jnp.sum(returned.reshape(EXPERTS, replicas, CAP, width), axis=1)
    else:
        expert_out = returned.reshape(EXPERTS, CAP, width)
    picked = jnp.take(expert_out.reshape(EXPERTS * CAP, width), slot_index, axis=0).reshape(
        tok_count, TOP, width
    )
    mixed = values + jnp.sum(gates[:, :, None] * picked, axis=1)
    embedded = mixed.astype(jnp.bfloat16)
    devices_all = plane * experts_axis
    seq_total = tok_count * devices_all // 256
    seq_hot = (jnp.arange(seq_total, dtype=jnp.int32)[:, None] == segments[None, :]).astype(
        jnp.bfloat16
    )
    seq_sums = jnp.dot(seq_hot, embedded, preferred_element_type=jnp.float32)
    seq_counts = jnp.sum(seq_hot.astype(jnp.float32), axis=1)
    total_sums, total_counts = lax.psum((seq_sums, seq_counts), ("dp", "tensor", "expert"))
    pooled = total_sums / total_counts[:, None]
    return (embedded, pooled)


def solution(mesh):
    placed = (
        P(("dp", "tensor", "expert"), None),
        P(("dp", "tensor", "expert"), None),
        P(("dp", "tensor", "expert"), None),
        P(("dp", "tensor", "expert")),
        P("expert", None, ("dp", "tensor")),
        P("expert", None, ("dp", "tensor")),
        P("expert", ("dp", "tensor"), None),
    )
    return jax.shard_map(
        shards,
        mesh=mesh,
        in_specs=placed,
        out_specs=(P(("dp", "tensor", "expert"), None), P()),
        check_vma=False,
    )
```

profile of v0, /device:TPU:8, one launch (start us, length us, event | category | flops | bytes accessed | tf_op | source)
XLA Modules:
  0.0 401.1 jit_solution(3369024853161112235)
XLA Ops:
  7.2 0.0 all-gather.2.cloned.1.call-start
  7.2 0.8 copy.29
  8.0 0.1 reshape.84
  8.1 0.1 fusion.19
  8.2 0.2 reduce_window_sum.11
  8.4 0.2 select_reduce_fusion
  8.6 0.1 reduce_sum.50
  8.7 0.1 copy.30
  8.8 0.7 compare_and_fusion
  9.5 0.1 convert_reduce_fusion
  9.6 1.1 fusion.14
  10.7 1.4 convolution_convert_fusion
  12.1 25.6 %all_to_all.14 = bf16[4,48,2304]{2,1,0:T(8,128)(2,1)S(1)} all-to-all(bf16[4,48,2304]{2,1,0:T(8,128)(2,1)S(1)} %bitcast.60), channel_id=1, replica_groups=mesh['dp'=4,'tensor'=2,'expert'=4] {'expert'}, dimensions={0} | all-to-all | bytes 1769472 | tf_op jit(solution)/shard_map/all_to_all | solution.py:62
  37.8 1.0 copy.32
  38.7 0.0 all-gather.2.cloned.1.call-update
  38.7 0.0 all-reduce.6.cloned.1.call-start
  38.8 49.3 %all-gather.2.cloned.1.call-done = bf16[32,2,24,2304]{3,2,0,1:T(8,128)(2,1)} async-done(((bf16[4,2,24,2304]{3,2,0,1:T(8,128)(2,1)}), bf16[32,2,24,2304]{3,2,0,1:T(8,128)(2,1)}) %all-gather.2.cloned.1.call-update) | async-done | bytes 7077904 | tf_op jit(solution)/shard_map/all_gather | solution.py:65
  88.0 11.1 %fusion.2 = f32[2,32,24,960]{3,2,1,0:T(8,128)S(1)} fusion(bf16[32,2,24,2304]{3,2,0,1:T(8,128)(2,1)} %all-gather.2.cloned.1.call-done, bf16[2,2304,960]{1,2,0:T(8,128)(2,1)} %param.12), kind=kOutput, calls=%fused_computation.3 | convolution fusion | flops 6794772480 | bytes 21823488 | tf_op jit(solution)/shard_map/nacd,adf->nacf/dot_general | solution.py:46
  99.1 13.0 %fusion.8 = bf16[32,2,24,960]{3,2,0,1:T(8,128)(2,1)S(1)} fusion(f32[2,32,24,960]{3,2,1,0:T(8,128)S(1)} %fusion.2, bf16[32,2,24,2304]{3,2,0,1:T(8,128)(2,1)} %all-gather.2.cloned.1.call-done, bf16[2,2304,960]{1,2,0:T(8,128)(2,1)} %param.11), kind=kOutput, calls=%fused_computation.9 | convolution fusion | flops 6803619840 | bytes 24772608 | tf_op jit(solution)/shard_map/nacd,adf->nacf/dot_general | solution.py:45
  112.2 12.9 %convert_bitcast_fusion = bf16[32,2,24,2304]{3,2,0,1:T(8,128)(2,1)} fusion(bf16[32,2,24,960]{3,2,0,1:T(8,128)(2,1)S(1)} %fusion.8, bf16[2,960,2304]{2,1,0:T(8,128)(2,1)} %param.13), kind=kOutput, calls=%fused_computation.7 | convolution fusion | flops 6798311424 | bytes 18874368 | tf_op jit(solution)/shard_map/nacf,afd->nacd/dot_general | solution.py:68
  125.0 0.0 all-reduce.6.cloned.1.call-update
  125.1 0.6 copy-done.5
  125.7 0.6 dynamic-slice
  126.9 111.2 %all-reduce.6.cloned.1.call-done = bf16[32,2,24,2304]{3,2,0,1:T(8,128)(2,1)} async-done(((bf16[32,2,24,2304]{3,2,0,1:T(8,128)(2,1)}), bf16[32,2,24,2304]{3,2,0,1:T(8,128)(2,1)}) %all-reduce.6.cloned.1.call-update) | async-done | bytes 7077904
  238.1 1.2 constant_dynamic-slice_fusion
  239.3 1.0 copy.33
  240.3 5.1 %all-to-all-start.1 = ((bf16[4,2,24,2304]{3,2,1,0:T(8,128)(2,1)}), bf16[4,2,24,2304]{3,2,1,0:T(8,128)(2,1)S(1)}, u32[]{:S(2)}, u32[]{:S(2)}) async-start(bf16[4,2,24,2304]{3,2,1,0:T(8,128)(2,1)} %copy.33), calls=%async_computation.1 | async-start | bytes 1769472 | tf_op jit(solution)/shard_map/all_to_all | solution.py:75
  245.4 0.0 all-reduce.4.cloned.1.call-start
  245.4 0.1 copy.34
  245.5 0.1 mul.61
  245.7 0.1 copy.31
  245.8 0.1 copy.28
  245.9 18.3 %all-to-all-done.1 = bf16[4,2,24,2304]{3,2,1,0:T(8,128)(2,1)S(1)} async-done(((bf16[4,2,24,2304]{3,2,1,0:T(8,128)(2,1)}), bf16[4,2,24,2304]{3,2,1,0:T(8,128)(2,1)S(1)}, u32[]{:S(2)}, u32[]{:S(2)}) %all-to-all-start.1) | async-done | bytes 884768 | tf_op jit(solution)/shard_map/all_to_all | solution.py:75
  264.3 0.2 bitcast_convert_fusion
  264.4 0.0 copy-start
  264.4 0.0 copy-start.4
  264.5 1.1 gather_fusion
  265.5 0.7 gather.7
  266.2 3.2 multiply_reduce_fusion
  269.4 0.1 fusion.16
  269.5 0.0 copy-start.1
  269.5 0.8 fusion.22
  270.3 0.0 all-reduce.4.cloned.1.call-update
  270.3 0.1 convert_reduce_fusion.1
  270.5 41.4 %psum.15 = f32[8]{0:T(128)S(1)} all-reduce(f32[8]{0:T(128)S(1)} %convert_reduce_fusion.1), channel_id=1, replica_groups=mesh['dp'=4,'tensor'=2,'expert'=4] {'dp','tensor','expert'}, use_global_device_ids=true, to_apply=%region_8.9 | all-reduce | flops 8 | bytes 64 | tf_op jit(solution)/shard_map/psum | solution.py:94
  311.9 81.1 %all-reduce.4.cloned.1.call-done = f32[8,2304]{1,0:T(8,128)} async-done(((f32[8,2304]{1,0:T(8,128)}), f32[8,2304]{1,0:T(8,128)}) %all-reduce.4.cloned.1.call-update) | async-done | bytes 73744 | tf_op jit(solution)/shard_map/psum | solution.py:94
  393.0 1.6 broadcast_divide_fusion
  394.6 0.0 copy-done.1
  (11 shorter events, 0.0 us)
Async XLA Ops:
  7.2 80.9 %all-gather.2.cloned.1.call-start = ((), (), s32[]{:S(2)}) async-start(), calls=%async_computation.2 | async-start | bytes 7962624 | tf_op jit(solution)/shard_map/all_gather | solution.py:65
  38.7 199.4 %all-reduce.6.cloned.1.call-start = ((), (), s32[]{:S(2)}) async-start(), calls=%async_computation.4 | async-start | bytes 14155776
  125.0 0.7 copy-start.5
  125.0 120.4 %copy-start.2 = (s32[64,2]{0,1:T(2,128)S(1)}, s32[64,2]{0,1:T(2,128)}, u32[]{:S(2)}) copy-start(s32[64,2]{0,1:T(2,128)} %param.8) | copy-start | bytes 1540
  125.0 120.8 %copy-start.3 = (f32[64,2]{0,1:T(2,128)S(1)}, f32[64,2]{0,1:T(2,128)}, u32[]{:S(2)}) copy-start(f32[64,2]{0,1:T(2,128)} %param.9) | copy-start | bytes 1540
  240.3 24.0 %all-to-all-start.1 = ((bf16[4,2,24,2304]{3,2,1,0:T(8,128)(2,1)}), bf16[4,2,24,2304]{3,2,1,0:T(8,128)(2,1)S(1)}, u32[]{:S(2)}, u32[]{:S(2)}) async-start(bf16[4,2,24,2304]{3,2,1,0:T(8,128)(2,1)} %copy.33), calls=%async_computation.1 | async-start | bytes 1769472 | tf_op jit(solution)/shard_map/all_to_all | solution.py:75
  245.4 147.5 %all-reduce.4.cloned.1.call-start = ((), (), s32[]{:S(2)}) async-start(), calls=%async_computation.3 | async-start | bytes 147456 | tf_op jit(solution)/shard_map/psum | solution.py:94
  264.4 5.0 %copy-start = (bf16[64,2304]{1,0:T(8,128)(2,1)S(1)}, bf16[64,2304]{1,0:T(8,128)(2,1)}, u32[]{:S(2)}) copy-start(bf16[64,2304]{1,0:T(8,128)(2,1)} %param.7) | copy-start | bytes 884740
  264.4 5.1 %copy-start.4 = (s32[64]{0:T(128)S(1)}, s32[64]{0:T(128)}, u32[]{:S(2)}) copy-start(s32[64]{0:T(128)} %param.10) | copy-start | bytes 772
  269.5 125.1 %copy-start.1 = (bf16[64,2304]{1,0:T(8,128)(2,1)}, bf16[64,2304]{1,0:T(8,128)(2,1)S(1)}, u32[]{:S(2)}) copy-start(bf16[64,2304]{1,0:T(8,128)(2,1)S(1)} %fusion.16) | copy-start | bytes 884740
Sparse Core Ops, SparseCore 0:
  38.9 49.1 all-gather.1
  125.2 112.8 all-reduce.5
  270.5 122.4 all-reduce.3
where the time goes:
time: 402 us; the launch traced here: 401 us
  waiting for transfers between devices  260 us (65%)
  blocking collectives  67 us (17%)
  matrix products  39.2 us (10%)
  between operations  14.6 us (4%)
  local copies, waits for them, and re-layouts  7.73 us (2%)
  other arithmetic  7.49 us (2%)
  starting transfers between devices  5.22 us (1%)
    unnamed x4, waiting for transfers between devices  111 us
    psum x1, waiting for transfers between devices, shards(): lax.psum((seq_sums, seq_counts), ('dp', 'tensor', 'expert'))  81.1 us
    all_gather x1, waiting for transfers between devices, shards(): lax.all_gather(local_rows, ('dp', 'tensor'), axis=0, tiled=True)  49.3 us
    psum x1, blocking collectives, shards(): lax.psum((seq_sums, seq_counts), ('dp', 'tensor', 'expert'))  41.4 us
    all_to_all x1, blocking collectives, shards(): lax.all_to_all(send_rows, 'expert', split_axis=0, concat_axis=0, tiled=True)  25.6 us
    all_to_all x1, waiting for transfers between devices, shards(): lax.all_to_all(summed, 'expert', split_axis=0, concat_axis=0, tiled=True)  18.3 us
    dot_general x1, matrix products, expert_hidden(): jnp.einsum('nacd,adf->nacf', row_block, w_gate, preferred_element_type=jn...  13 us
    dot_general x1, matrix products, shards(): jnp.einsum('nacf,afd->nacd', hidden, w_down, preferred_element_type=jnp.f...  12.9 us
  transfers between devices with their start and end apart: 4, of which 4 were waited for; matrix products, arithmetic and copies ran while one was open for 0% of the time, Pallas kernels for 0%

commit v1 on v0

--- a/solution.py
+++ b/solution.py
@@ -91,7 +91,9 @@
     )
     seq_sums = jnp.dot(seq_hot, embedded, preferred_element_type=jnp.float32)
     seq_counts = jnp.sum(seq_hot.astype(jnp.float32), axis=1)
-    total_sums, total_counts = lax.psum((seq_sums, seq_counts), ("dp", "tensor", "expert"))
+    total_sums, total_counts = lax.psum(
+        lax.psum((seq_sums, seq_counts), ("tensor", "expert")), "dp"
+    )
     pooled = total_sums / total_counts[:, None]
     return (embedded, pooled)
 

time: 402 us -> 377 us (0.938)
  blocking collectives: 67 us -> 48.5 us
  waiting for transfers between devices: 260 us -> 252 us
    psum x1 -> x2, blocking collectives: 41.4 us -> 22.9 us  [the longest x1 13.1 us: shards(): lax.psum((seq_sums, seq_counts), ('tensor', 'expert'))]
    psum x1 -> x2, waiting for transfers between devices: 81.1 us -> 73.6 us  [the longest x1 53.2 us: shards(): lax.psum((seq_sums, seq_counts), ('tensor', 'expert'))]
    unnamed x4 -> x5, waiting for transfers between devices: 111 us -> 111 us
  transfers between devices with their start and end apart: 4 -> 5, of which waited for: 4 -> 5; matrix products, arithmetic and copies ran while one was open for 0% -> 0% of each run, Pallas kernels for 0% -> 0%
where the time goes in v1:
time: 377 us; the launch traced here: 375 us
  waiting for transfers between devices  252 us (67%)
  blocking collectives  48.5 us (13%)
  matrix products  39.2 us (10%)
  between operations  14.6 us (4%)
  local copies, waits for them, and re-layouts  7.73 us (2%)
  other arithmetic  7.49 us (2%)
  starting transfers between devices  5.26 us (1%)
    unnamed x5, waiting for transfers between devices  111 us
    psum x1, waiting for transfers between devices, shards(): lax.psum((seq_sums, seq_counts), ('tensor', 'expert'))  53.2 us
    all_gather x1, waiting for transfers between devices, shards(): lax.all_gather(local_rows, ('dp', 'tensor'), axis=0, tiled=True)  49.3 us
    all_to_all x1, blocking collectives, shards(): lax.all_to_all(send_rows, 'expert', split_axis=0, concat_axis=0, tiled=True)  25.6 us
    psum x1, waiting for transfers between devices, shards(): lax.psum(lax.psum((seq_sums, seq_counts), ('tensor', 'expert')), 'dp')  20.4 us
    all_to_all x1, waiting for transfers between devices, shards(): lax.all_to_all(summed, 'expert', split_axis=0, concat_axis=0, tiled=True)  18.3 us
    psum x1, blocking collectives, shards(): lax.psum((seq_sums, seq_counts), ('tensor', 'expert'))  13.1 us
    dot_general x1, matrix products, expert_hidden(): jnp.einsum('nacd,adf->nacf', row_block, w_gate, preferred_element_type=jn...  13 us
  transfers between devices with their start and end apart: 5, of which 5 were waited for; matrix products, arithmetic and copies ran while one was open for 0% of the time, Pallas kernels for 0%

profile of v1, /device:TPU:8, one launch (start us, length us, event | category | flops | bytes accessed | tf_op | source)
XLA Modules:
  0.0 375.1 jit_solution(13139870784524885286)
XLA Ops:
  7.2 0.0 all-gather.2.cloned.1.call-start
  7.2 0.8 copy.29
  8.0 0.1 reshape.84
  8.1 0.1 fusion.19
  8.2 0.2 reduce_window_sum.11
  8.4 0.2 select_reduce_fusion
  8.6 0.1 reduce_sum.50
  8.7 0.1 copy.30
  8.8 0.7 compare_and_fusion
  9.5 0.1 convert_reduce_fusion
  9.6 1.1 fusion.14
  10.7 1.4 convolution_convert_fusion
  12.1 25.6 %all_to_all.14 = bf16[4,48,2304]{2,1,0:T(8,128)(2,1)S(1)} all-to-all(bf16[4,48,2304]{2,1,0:T(8,128)(2,1)S(1)} %bitcast.60), channel_id=1, replica_groups=mesh['dp'=4,'tensor'=2,'expert'=4] {'expert'}, dimensions={0} | all-to-all | bytes 1769472 | tf_op jit(solution)/shard_map/all_to_all | solution.py:62
  37.8 1.0 copy.32
  38.7 0.0 all-gather.2.cloned.1.call-update
  38.7 0.0 all-reduce.9.cloned.1.call-start
  38.8 49.3 %all-gather.2.cloned.1.call-done = bf16[32,2,24,2304]{3,2,0,1:T(8,128)(2,1)} async-done(((bf16[4,2,24,2304]{3,2,0,1:T(8,128)(2,1)}), bf16[32,2,24,2304]{3,2,0,1:T(8,128)(2,1)}) %all-gather.2.cloned.1.call-update) | async-done | bytes 7077904 | tf_op jit(solution)/shard_map/all_gather | solution.py:65
  88.0 11.1 %fusion.2 = f32[2,32,24,960]{3,2,1,0:T(8,128)S(1)} fusion(bf16[32,2,24,2304]{3,2,0,1:T(8,128)(2,1)} %all-gather.2.cloned.1.call-done, bf16[2,2304,960]{1,2,0:T(8,128)(2,1)} %param.12), kind=kOutput, calls=%fused_computation.3 | convolution fusion | flops 6794772480 | bytes 21823488 | tf_op jit(solution)/shard_map/nacd,adf->nacf/dot_general | solution.py:46
  99.1 13.0 %fusion.8 = bf16[32,2,24,960]{3,2,0,1:T(8,128)(2,1)S(1)} fusion(f32[2,32,24,960]{3,2,1,0:T(8,128)S(1)} %fusion.2, bf16[32,2,24,2304]{3,2,0,1:T(8,128)(2,1)} %all-gather.2.cloned.1.call-done, bf16[2,2304,960]{1,2,0:T(8,128)(2,1)} %param.11), kind=kOutput, calls=%fused_computation.9 | convolution fusion | flops 6803619840 | bytes 24772608 | tf_op jit(solution)/shard_map/nacd,adf->nacf/dot_general | solution.py:45
  112.2 12.9 %convert_bitcast_fusion = bf16[32,2,24,2304]{3,2,0,1:T(8,128)(2,1)} fusion(bf16[32,2,24,960]{3,2,0,1:T(8,128)(2,1)S(1)} %fusion.8, bf16[2,960,2304]{2,1,0:T(8,128)(2,1)} %param.13), kind=kOutput, calls=%fused_computation.7 | convolution fusion | flops 6798311424 | bytes 18874368 | tf_op jit(solution)/shard_map/nacf,afd->nacd/dot_general | solution.py:68
  125.0 0.0 all-reduce.9.cloned.1.call-update
  125.1 0.6 copy-done.5
  125.7 0.6 dynamic-slice
  126.9 111.2 %all-reduce.9.cloned.1.call-done = bf16[32,2,24,2304]{3,2,0,1:T(8,128)(2,1)} async-done(((bf16[32,2,24,2304]{3,2,0,1:T(8,128)(2,1)}), bf16[32,2,24,2304]{3,2,0,1:T(8,128)(2,1)}) %all-reduce.9.cloned.1.call-update) | async-done | bytes 7077904
  238.1 1.2 constant_dynamic-slice_fusion
  239.3 1.0 copy.33
  240.3 5.1 %all-to-all-start.1 = ((bf16[4,2,24,2304]{3,2,1,0:T(8,128)(2,1)}), bf16[4,2,24,2304]{3,2,1,0:T(8,128)(2,1)S(1)}, u32[]{:S(2)}, u32[]{:S(2)}) async-start(bf16[4,2,24,2304]{3,2,1,0:T(8,128)(2,1)} %copy.33), calls=%async_computation.1 | async-start | bytes 1769472 | tf_op jit(solution)/shard_map/all_to_all | solution.py:75
  245.4 0.1 copy.34
  245.5 0.1 mul.61
  245.7 0.1 copy.31
  245.8 0.1 copy.28
  245.9 18.3 %all-to-all-done.1 = bf16[4,2,24,2304]{3,2,1,0:T(8,128)(2,1)S(1)} async-done(((bf16[4,2,24,2304]{3,2,1,0:T(8,128)(2,1)}), bf16[4,2,24,2304]{3,2,1,0:T(8,128)(2,1)S(1)}, u32[]{:S(2)}, u32[]{:S(2)}) %all-to-all-start.1) | async-done | bytes 884768 | tf_op jit(solution)/shard_map/all_to_all | solution.py:75
  264.3 0.2 bitcast_convert_fusion
  264.5 1.1 gather_fusion
  265.5 0.7 gather.7
  266.2 3.2 multiply_reduce_fusion
  269.4 0.1 fusion.16
  269.5 0.0 copy-start.1
  269.5 0.8 fusion.22
  270.3 0.0 all-reduce.5.cloned.1.call-update
  270.3 0.0 all-reduce.7.cloned.1.call-start
  270.4 53.2 %all-reduce.5.cloned.1.call-done = f32[8,2304]{1,0:T(8,128)} async-done(((f32[8,2304]{1,0:T(8,128)}), f32[8,2304]{1,0:T(8,128)}) %all-reduce.5.cloned.1.call-update) | async-done | bytes 73744 | tf_op jit(solution)/shard_map/psum | solution.py:95
  323.6 0.0 all-reduce.7.cloned.1.call-update
  323.6 0.1 convert_reduce_fusion.1
  323.7 13.1 %psum.30 = f32[8]{0:T(128)S(1)} all-reduce(f32[8]{0:T(128)S(1)} %convert_reduce_fusion.1), channel_id=1, replica_groups=mesh['dp'=4,'tensor'=2,'expert'=4] {'tensor','expert'}, use_global_device_ids=true, to_apply=%region_9.10 | all-reduce | flops 8 | bytes 64 | tf_op jit(solution)/shard_map/psum | solution.py:95
  336.8 9.8 %psum.31 = f32[8]{0:T(128)S(1)} all-reduce(f32[8]{0:T(128)S(1)} %psum.30), channel_id=1, replica_groups=mesh['dp'=4,'tensor'=2,'expert'=4] {'dp'}, use_global_device_ids=true, to_apply=%region_10.11 | all-reduce | flops 8 | bytes 64 | tf_op jit(solution)/shard_map/psum | solution.py:94
  346.6 20.4 %all-reduce.7.cloned.1.call-done = f32[8,2304]{1,0:T(8,128)} async-done(((f32[8,2304]{1,0:T(8,128)}), f32[8,2304]{1,0:T(8,128)}) %all-reduce.7.cloned.1.call-update) | async-done | bytes 73744 | tf_op jit(solution)/shard_map/psum | solution.py:94
  367.0 1.6 broadcast_divide_fusion
  (15 shorter events, 0.0 us)
Async XLA Ops:
  7.2 80.9 %all-gather.2.cloned.1.call-start = ((), (), s32[]{:S(2)}) async-start(), calls=%async_computation.2 | async-start | bytes 7962624 | tf_op jit(solution)/shard_map/all_gather | solution.py:65
  38.7 199.4 %all-reduce.9.cloned.1.call-start = ((), (), s32[]{:S(2)}) async-start(), calls=%async_computation.5 | async-start | bytes 14155776
  125.0 0.7 copy-start.5
  125.0 120.4 %copy-start.2 = (s32[64,2]{0,1:T(2,128)S(1)}, s32[64,2]{0,1:T(2,128)}, u32[]{:S(2)}) copy-start(s32[64,2]{0,1:T(2,128)} %param.8) | copy-start | bytes 1540
  125.0 120.8 %copy-start.3 = (f32[64,2]{0,1:T(2,128)S(1)}, f32[64,2]{0,1:T(2,128)}, u32[]{:S(2)}) copy-start(f32[64,2]{0,1:T(2,128)} %param.9) | copy-start | bytes 1540
  240.3 24.0 %all-to-all-start.1 = ((bf16[4,2,24,2304]{3,2,1,0:T(8,128)(2,1)}), bf16[4,2,24,2304]{3,2,1,0:T(8,128)(2,1)S(1)}, u32[]{:S(2)}, u32[]{:S(2)}) async-start(bf16[4,2,24,2304]{3,2,1,0:T(8,128)(2,1)} %copy.33), calls=%async_computation.1 | async-start | bytes 1769472 | tf_op jit(solution)/shard_map/all_to_all | solution.py:75
  245.4 78.1 %all-reduce.5.cloned.1.call-start = ((), (), s32[]{:S(2)}) async-start(), calls=%async_computation.3 | async-start | bytes 147456 | tf_op jit(solution)/shard_map/psum | solution.py:95
  264.4 5.0 %copy-start = (bf16[64,2304]{1,0:T(8,128)(2,1)S(1)}, bf16[64,2304]{1,0:T(8,128)(2,1)}, u32[]{:S(2)}) copy-start(bf16[64,2304]{1,0:T(8,128)(2,1)} %param.7) | copy-start | bytes 884740
  264.4 5.1 %copy-start.4 = (s32[64]{0:T(128)S(1)}, s32[64]{0:T(128)}, u32[]{:S(2)}) copy-start(s32[64]{0:T(128)} %param.10) | copy-start | bytes 772
  269.5 99.1 %copy-start.1 = (bf16[64,2304]{1,0:T(8,128)(2,1)}, bf16[64,2304]{1,0:T(8,128)(2,1)S(1)}, u32[]{:S(2)}) copy-start(bf16[64,2304]{1,0:T(8,128)(2,1)S(1)} %fusion.16) | copy-start | bytes 884740
  270.3 96.7 %all-reduce.7.cloned.1.call-start = ((), (), s32[]{:S(2)}) async-start(), calls=%async_computation.4 | async-start | bytes 147456 | tf_op jit(solution)/shard_map/psum | solution.py:94
Sparse Core Ops, SparseCore 0:
  38.9 49.1 all-gather.1
  125.2 112.8 all-reduce.8
  270.5 53.0 all-reduce.4
  326.6 40.3 all-reduce.6
